TPU v7x, 32 devices: a whole 2x2x4 slice. The times are simulated.
32 devices in a mesh: row: 8 (over y, x, core), col: 4 (over z).
Axes of the slice: x: 2, y: 2, z: 4, core: 2. Of those that a mesh axis runs over, the one named last changes fastest.
Arguments:
- vector_panel: bfloat16 [8192, 256], P(('row', 'col')), may hold values from -6 to 6
- block_tiles: bfloat16 [3072, 128, 128], P(('row', 'col')), may hold values from -0.0625 to 0.0625
- tile_rows: int32 [3072], P(('row', 'col')), may hold values from 0 to 63, as said below
- tile_cols: int32 [3072], P(('row', 'col')), may hold values from 0 to 63, as said below
- owner_counts: int32 [32], P(('row', 'col')), may hold values from 1 to 96, as said below
Outputs:
- filtered: bfloat16 [8192, 256], P(('row', 'col'))
Inputs may be any that keep to these rules, and one draw needn't show every extreme that they name: The live slots of owner (row index p, col index q) hold distinct pairs (tile_rows, tile_cols) with tile_rows <= tile_cols, tile_rows in p * 2 * 4 to (p + 1) * 2 * 4 - 1 and tile_cols // 2 % 4 = q; slots past the owner's count repeat its first pair and are ignored. `tile_cols`: see tile_rows. `owner_counts`: some owner fills all 96 slots.
All inputs are finite; a program needn't handle non-finite values.
Results may differ from a plain program's by a relative error of at most 0.022.
Values may be sent and summed in bfloat16 or wider, within the bound.
No kernel may reach another device: no remote copies, remote signals or barrier semaphores. Data moves between devices by JAX's collectives and lax.ppermute only.
A program may use at most 128 MiB of HBM per device.

v0:
```python
import jax
import jax.numpy as jnp
from jax import lax
from jax.sharding import PartitionSpec as P

BS = 128
center_shift = 0.25
half_width = 1.25


def apply_blocks(
    panel, block_tiles, row_slot, set_slot, row_select, set_select, range_blocks, set_blocks
):
    width = panel.shape[1]
    gathered_set = lax.all_gather(panel, "row", axis=0, tiled=True).reshape(set_blocks, BS, width)
    picked_set = jnp.take(gathered_set, set_slot, axis=0)
    upper = jnp.einsum("sij,sjw->siw", block_tiles, picked_set, preferred_element_type=jnp.float32)
    upper_sum = jnp.einsum(
        "as,siw->aiw", row_select, upper, precision=lax.Precision.HIGHEST
    ).astype(jnp.bfloat16)
    own_upper = lax.psum_scatter(
        upper_sum.reshape(range_blocks * BS, width), "col", scatter_dimension=0, tiled=True
    ).astype(jnp.float32)
    gathered_range = lax.all_gather(panel, "col", axis=0, tiled=True).reshape(
        range_blocks, BS, width
    )
    picked_range = jnp.take(gathered_range, row_slot, axis=0)
    lower = jnp.einsum(
        "sji,sjw->siw", block_tiles, picked_range, preferred_element_type=jnp.float32
    )
    lower_sum = jnp.einsum(
        "bs,siw->biw", set_select, lower, precision=lax.Precision.HIGHEST
    ).astype(jnp.bfloat16)
    own_lower = lax.psum_scatter(
        lower_sum.reshape(set_blocks * BS, width), "row", scatter_dimension=0, tiled=True
    ).astype(jnp.float32)
    return own_upper + own_lower


def per_device(vector_panel, block_tiles, tile_rows, tile_cols, owner_counts):
    n_rows = lax.axis_size("row")
    n_cols = lax.axis_size("col")
    row_index = lax.axis_index("row")
    panel_blocks = vector_panel.shape[0] // BS
    slots = block_tiles.shape[0]
    range_blocks = panel_blocks * n_cols
    set_blocks = panel_blocks * n_rows
    row_slot = tile_rows - row_index * range_blocks
    shard_of = tile_cols // panel_blocks
    set_slot = shard_of // n_cols * panel_blocks + tile_cols % panel_blocks
    live_slots = jnp.arange(slots, dtype=jnp.int32) < owner_counts[0]
    row_select = (
        (row_slot[None, :] == jnp.arange(range_blocks, dtype=jnp.int32)[:, None])
        & live_slots[None, :]
    ).astype(jnp.float32)
    set_select = (
        (set_slot[None, :] == jnp.arange(set_blocks, dtype=jnp.int32)[:, None])
        & live_slots[None, :]
    ).astype(jnp.float32)

    def operate(panel):
        return apply_blocks(
            panel, block_tiles, row_slot, set_slot, row_select, set_select, range_blocks, set_blocks
        )

    start_f = vector_panel.astype(jnp.float32)
    hx = operate(vector_panel)
    first_step = ((hx - center_shift * start_f) / half_width).astype(jnp.bfloat16)
    first_f = first_step.astype(jnp.float32)
    hfirst = operate(first_step)
    filtered = 2.0 * (hfirst - center_shift * first_f) / half_width - start_f
    return filtered.astype(jnp.bfloat16)


def solution(mesh):
    in_specs = (
        P(("row", "col"), None),
        P(("row", "col"), None, None),
        P(("row", "col")),
        P(("row", "col")),
        P(("row", "col")),
    )
    out_specs = P(("row", "col"), None)
    return jax.shard_map(
        per_device, mesh=mesh, in_specs=in_specs, out_specs=out_specs, check_vma=False
    )
```

profile of v0, /device:TPU:0, one launch (start us, length us, event | category | flops | bytes accessed | tf_op | source)
XLA Modules:
  0.0 249.5 jit_solution(10400839575763858375)
XLA Ops:
  8.1 19.4 %all_gather.13 = bf16[1024,256]{1,0:T(8,128)(2,1)} all-gather(bf16[256,256]{1,0:T(8,128)(2,1)} %param.9), channel_id=1, replica_groups=mesh['row'=8,'col'=4] {'col'}, dimensions={0}, use_global_device_ids=true | all-gather | bytes 655360 | tf_op jit(solution)/shard_map/all_gather | solution.py:24
  27.5 7.0 %gather_fusion.1 = bf16[96,128,256]{2,1,0:T(8,128)(2,1)} fusion(bf16[8,128,256]{2,1,0:T(8,128)(2,1)} %bitcast.42, s32[1024]{0:T(1024)S(1)} %pad_clamp_fusion), kind=kCustom, calls=%fused_computation.1.clone | custom fusion | bytes 12583296 | tf_op jit(solution)/shard_map/jit(_take)/gather | solution.py:27
  34.5 9.3 %fusion.12 = f32[96,256,128]{2,1,0:T(8,128)} fusion(bf16[96,128,128]{2,1,0:T(8,128)(2,1)S(1)} %copy-done, bf16[96,128,256]{2,1,0:T(8,128)(2,1)} %gather_fusion.1, pred[96]{0:T(512)(128)(4,1)S(1)} %get-tuple-element.9), kind=kOutput, calls=%fused_computation.16 | convolution fusion | flops 808452096 | bytes 22020192 | tf_op jit(solution)/shard_map/sji,sjw->siw/dot_general | solution.py:28
  43.8 12.7 %copy.11 = f32[96,256,128]{1,0,2:T(8,128)} copy(f32[96,256,128]{2,1,0:T(8,128)} %fusion.12) | data formatting | bytes 25165824 | tf_op jit(solution)/shard_map/sji,sjw->siw/dot_general | solution.py:28
  57.2 7.1 %fusion.24 = bf16[16,128,256]{2,0,1:T(8,128)(2,1)S(1)} fusion(f32[96,256,128]{1,0,2:T(8,128)} %copy.11, s32[96]{0:T(128)S(1)} %get-tuple-element.8, pred[96]{0:T(512)(128)(4,1)S(1)} %iota_compare_fusion.2), kind=kOutput, calls=%fused_computation.28 | convolution fusion | flops 604507136 | bytes 13631968 | tf_op jit(solution)/shard_map/bs,siw->biw/dot_general | solution.py:31
  64.3 1.3 copy.7
  65.9 7.3 %gather_fusion = bf16[96,128,256]{2,1,0:T(8,128)(2,1)} fusion(bf16[16,128,256]{2,1,0:T(8,128)(2,1)} %bitcast.44, s32[1024]{0:T(1024)S(1)} %pad_clamp_fusion.1), kind=kCustom, calls=%fused_computation.clone | custom fusion | bytes 12583296 | tf_op jit(solution)/shard_map/jit(_take)/gather | solution.py:16
  73.2 9.5 %fusion.14 = f32[96,256,128]{2,1,0:T(8,128)} fusion(bf16[96,128,128]{2,1,0:T(8,128)(2,1)S(1)} %copy-done, bf16[96,128,256]{2,1,0:T(8,128)(2,1)} %gather_fusion, pred[96]{0:T(512)(128)(4,1)S(1)} %get-tuple-element.6), kind=kOutput, calls=%fused_computation.18 | convolution fusion | flops 808452096 | bytes 22020192 | tf_op jit(solution)/shard_map/sij,sjw->siw/dot_general | solution.py:17
  82.7 12.7 %copy.10 = f32[96,256,128]{1,0,2:T(8,128)} copy(f32[96,256,128]{2,1,0:T(8,128)} %fusion.14) | data formatting | bytes 25165824 | tf_op jit(solution)/shard_map/sij,sjw->siw/dot_general | solution.py:17
  95.4 7.1 %fusion.30 = bf16[8,128,256]{2,0,1:T(8,128)(2,1)S(1)} fusion(f32[96,256,128]{1,0,2:T(8,128)} %copy.10, s32[96]{0:T(128)S(1)} %get-tuple-element.10, pred[96]{0:T(512)(128)(4,1)S(1)} %iota_compare_fusion.2), kind=kOutput, calls=%fused_computation.30 | convolution fusion | flops 302253568 | bytes 13107680 | tf_op jit(solution)/shard_map/as,siw->aiw/dot_general | solution.py:18
  103.6 22.1 %reduce-scatter.5.cloned.1.call-done = bf16[256,256]{1,0:T(8,128)(2,1)} async-done(((bf16[1024,256]{1,0:T(8,128)(2,1)}), bf16[256,256]{1,0:T(8,128)(2,1)}) %reduce-scatter.5.cloned.1.call-update) | async-done | bytes 131088 | tf_op jit(solution)/shard_map/reduce_scatter | solution.py:21
  125.6 1.7 fusion.38
  127.4 17.2 %all_gather.15 = bf16[1024,256]{1,0:T(8,128)(2,1)} all-gather(bf16[256,256]{1,0:T(8,128)(2,1)} %fusion.38), channel_id=1, replica_groups=mesh['row'=8,'col'=4] {'col'}, dimensions={0}, use_global_device_ids=true | all-gather | bytes 655360 | tf_op jit(solution)/shard_map/all_gather | solution.py:24
  144.6 7.0 %gather_fusion.3 = bf16[96,128,256]{2,1,0:T(8,128)(2,1)} fusion(bf16[8,128,256]{2,1,0:T(8,128)(2,1)} %bitcast.43, s32[1024]{0:T(1024)S(1)} %pad_clamp_fusion), kind=kCustom, calls=%fused_computation.3.clone | custom fusion | bytes 12583296 | tf_op jit(solution)/shard_map/jit(_take)/gather | solution.py:27
  151.5 9.3 %fusion.8 = f32[96,256,128]{2,1,0:T(8,128)} fusion(bf16[96,128,128]{2,1,0:T(8,128)(2,1)S(1)} %copy-done, bf16[96,128,256]{2,1,0:T(8,128)(2,1)} %gather_fusion.3, pred[96]{0:T(512)(128)(4,1)S(1)} %get-tuple-element.9), kind=kOutput, calls=%fused_computation.12 | convolution fusion | flops 808452096 | bytes 22020192 | tf_op jit(solution)/shard_map/sji,sjw->siw/dot_general | solution.py:28
  160.8 12.7 %copy.13 = f32[96,256,128]{1,0,2:T(8,128)} copy(f32[96,256,128]{2,1,0:T(8,128)} %fusion.8) | data formatting | bytes 25165824 | tf_op jit(solution)/shard_map/sji,sjw->siw/dot_general | solution.py:28
  173.5 7.1 %fusion.27 = bf16[16,128,256]{2,0,1:T(8,128)(2,1)S(1)} fusion(f32[96,256,128]{1,0,2:T(8,128)} %copy.13, s32[96]{0:T(128)S(1)} %get-tuple-element.8, pred[96]{0:T(512)(128)(4,1)S(1)} %iota_compare_fusion.2), kind=kOutput, calls=%fused_computation.29 | convolution fusion | flops 604507136 | bytes 13631968 | tf_op jit(solution)/shard_map/bs,siw->biw/dot_general | solution.py:31
  180.6 1.3 copy.9
  182.3 7.3 %gather_fusion.2 = bf16[96,128,256]{2,1,0:T(8,128)(2,1)} fusion(bf16[16,128,256]{2,1,0:T(8,128)(2,1)} %bitcast.45, s32[1024]{0:T(1024)S(1)} %pad_clamp_fusion.1), kind=kCustom, calls=%fused_computation.2.clone | custom fusion | bytes 12583296 | tf_op jit(solution)/shard_map/jit(_take)/gather | solution.py:16
  189.6 9.5 %fusion.10 = f32[96,256,128]{2,1,0:T(8,128)} fusion(bf16[96,128,128]{2,1,0:T(8,128)(2,1)S(1)} %copy-done, bf16[96,128,256]{2,1,0:T(8,128)(2,1)} %gather_fusion.2, pred[96]{0:T(512)(128)(4,1)S(1)} %get-tuple-element.6), kind=kOutput, calls=%fused_computation.14 | convolution fusion | flops 808452096 | bytes 22020192 | tf_op jit(solution)/shard_map/sij,sjw->siw/dot_general | solution.py:17
  199.0 12.7 %copy.12 = f32[96,256,128]{1,0,2:T(8,128)} copy(f32[96,256,128]{2,1,0:T(8,128)} %fusion.10) | data formatting | bytes 25165824 | tf_op jit(solution)/shard_map/sij,sjw->siw/dot_general | solution.py:17
  211.7 7.1 %fusion.33 = bf16[8,128,256]{2,0,1:T(8,128)(2,1)S(1)} fusion(f32[96,256,128]{1,0,2:T(8,128)} %copy.12, s32[96]{0:T(128)S(1)} %get-tuple-element.10, pred[96]{0:T(512)(128)(4,1)S(1)} %iota_compare_fusion.2), kind=kOutput, calls=%fused_computation.31 | convolution fusion | flops 302253568 | bytes 13107680 | tf_op jit(solution)/shard_map/as,siw->aiw/dot_general | solution.py:18
  219.8 21.2 %reduce-scatter.9.cloned.1.call-done = bf16[256,256]{1,0:T(8,128)(2,1)} async-done(((bf16[1024,256]{1,0:T(8,128)(2,1)}), bf16[256,256]{1,0:T(8,128)(2,1)}) %reduce-scatter.9.cloned.1.call-update) | async-done | bytes 131088 | tf_op jit(solution)/shard_map/reduce_scatter | solution.py:21
  241.0 1.7 fusion.39
  (33 shorter events, 4.2 us)
Async XLA Ops:
  6.5 28.0 %copy-start = (bf16[96,128,128]{2,1,0:T(8,128)(2,1)S(1)}, bf16[96,128,128]{2,1,0:T(8,128)(2,1)}, u32[]{:S(2)}) copy-start(bf16[96,128,128]{2,1,0:T(8,128)(2,1)} %param.10) | copy-start | bytes 9437188
  6.5 59.4 %all-gather.3.cloned.1.call-start = ((), (), s32[]{:S(2)}) async-start(), calls=%async_computation.4 | async-start | bytes 1179648 | tf_op jit(solution)/shard_map/all_gather | solution.py:15
  7.3 96.3 %reduce-scatter.7.cloned.1.call-start = ((), (), s32[]{:S(2)}) async-start(), calls=%async_computation.6 | async-start | bytes 1179648 | tf_op jit(solution)/shard_map/reduce_scatter | solution.py:34
  43.8 13.4 %copy-start.3 = (s32[96]{0:T(128)S(1)}, s32[96]{0:T(128)}, u32[]{:S(2)}) copy-start(s32[96]{0:T(128)} %param.12) | copy-start | bytes 1156
  65.7 60.0 %reduce-scatter.5.cloned.1.call-start = ((), (), s32[]{:S(2)}) async-start(), calls=%async_computation.5 | async-start | bytes 655360 | tf_op jit(solution)/shard_map/reduce_scatter | solution.py:21
  95.4 30.2 %copy-start.1 = (bf16[256,256]{1,0:T(8,128)(2,1)S(1)}, bf16[256,256]{1,0:T(8,128)(2,1)}, u32[]{:S(2)}) copy-start(bf16[256,256]{1,0:T(8,128)(2,1)} %param.9) | copy-start | bytes 393220
  103.5 78.8 %all-gather.5.cloned.1.call-start = ((), (), s32[]{:S(2)}) async-start(), calls=%async_computation.7 | async-start | bytes 1179648 | tf_op jit(solution)/shard_map/all_gather | solution.py:15
  127.4 92.4 %reduce-scatter.11.cloned.1.call-start = ((), (), s32[]{:S(2)}) async-start(), calls=%async_computation.9 | async-start | bytes 1179648 | tf_op jit(solution)/shard_map/reduce_scatter | solution.py:34
  182.0 59.0 %reduce-scatter.9.cloned.1.call-start = ((), (), s32[]{:S(2)}) async-start(), calls=%async_computation.8 | async-start | bytes 655360 | tf_op jit(solution)/shard_map/reduce_scatter | solution.py:21
  211.7 29.2 %copy-start.2 = (bf16[256,256]{1,0:T(8,128)(2,1)S(1)}, bf16[256,256]{1,0:T(8,128)(2,1)}, u32[]{:S(2)}) copy-start(bf16[256,256]{1,0:T(8,128)(2,1)} %fusion.38) | copy-start | bytes 393220
Sparse Core Ops, SparseCore 0:
  9.2 26.0 all-gather.2
  65.8 35.6 reduce-scatter.6
  103.8 21.8 reduce-scatter.4
  127.5 21.6 all-gather.4
  182.1 34.8 reduce-scatter.10
  219.9 21.0 reduce-scatter.8
where the time goes:
time: 251 us; the launch traced here: 250 us
  local copies, waits for them, and re-layouts  83.9 us (33%)
  matrix products  65.8 us (26%)
  waiting for transfers between devices  44.1 us (18%)
  blocking collectives  36.5 us (15%)
  between operations  14.2 us (6%)
  other arithmetic  4.28 us (2%)
    reduce_scatter x2, waiting for transfers between devices, apply_blocks(): lax.psum_scatter(upper_sum.reshape(range_blocks * BS, width), 'col', scat...  43.3 us
    all_gather x2, blocking collectives, apply_blocks(): lax.all_gather(panel, 'col', axis=0, tiled=True)  36.5 us
    dot_general x2, local copies, waits for them, and re-layouts, apply_blocks(): jnp.einsum('sij,sjw->siw', block_tiles, picked_set, preferred_element_typ...  25.5 us
    dot_general x2, local copies, waits for them, and re-layouts, apply_blocks(): jnp.einsum('sji,sjw->siw', block_tiles, picked_range, preferred_element_t...  25.4 us
    dot_general x2, matrix products, apply_blocks(): jnp.einsum('sij,sjw->siw', block_tiles, picked_set, preferred_element_typ...  18.9 us
    dot_general x2, matrix products, apply_blocks(): jnp.einsum('sji,sjw->siw', block_tiles, picked_range, preferred_element_t...  18.5 us
    gather x2, local copies, waits for them, and re-layouts, apply_blocks(): picked_set = jnp.take(gathered_set, set_slot, axis=0)  14.5 us
    dot_general x2, matrix products, apply_blocks(): jnp.einsum('as,siw->aiw', row_select, upper, precision=lax.Precision.HIGH...  14.2 us
  transfers between devices with their start and end apart: 6, of which 2 were waited for; matrix products, arithmetic and copies ran while one was open for 60% of the time, Pallas kernels for 0%

commit v1 on v0

--- a/solution.py
+++ b/solution.py
@@ -6,6 +6,27 @@
 BS = 128
 center_shift = 0.25
 half_width = 1.25
+
+
+def collect(x, axis, dim):
+    size, index, rows = (lax.axis_size(axis), lax.axis_index(axis), x.shape[dim])
+    right = [(i, (i + 1) % size) for i in range(size)]
+    left = [(i, (i - 1) % size) for i in range(size)]
+    out = jnp.zeros((*x.shape[:dim], size * rows, *x.shape[dim + 1 :]), x.dtype)
+    out = lax.dynamic_update_slice_in_dim(out, x, index * rows, axis=dim)
+    from_left = from_right = x
+    half = size // 2
+    for step in range(1, half + 1):
+        from_left = lax.ppermute(from_left, axis, right)
+        out = lax.dynamic_update_slice_in_dim(
+            out, from_left, (index - step) % size * rows, axis=dim
+        )
+        if step < size - half:
+            from_right = lax.ppermute(from_right, axis, left)
+            out = lax.dynamic_update_slice_in_dim(
+                out, from_right, (index + step) % size * rows, axis=dim
+            )
+    return out
 
 
 def apply_blocks(
@@ -21,9 +42,7 @@
     own_upper = lax.psum_scatter(
         upper_sum.reshape(range_blocks * BS, width), "col", scatter_dimension=0, tiled=True
     ).astype(jnp.float32)
-    gathered_range = lax.all_gather(panel, "col", axis=0, tiled=True).reshape(
-        range_blocks, BS, width
-    )
+    gathered_range = collect(panel, "col", 0).reshape(range_blocks, BS, width)
     picked_range = jnp.take(gathered_range, row_slot, axis=0)
     lower = jnp.einsum(
         "sji,sjw->siw", block_tiles, picked_range, preferred_element_type=jnp.float32

time: 251 us -> 243 us (0.968)
  blocking collectives: 36.5 us -> 0 us
  waiting for transfers between devices: 44.1 us -> 56.1 us
  starting transfers between devices: 0.65 us -> 9.02 us
  local copies, waits for them, and re-layouts: 83.9 us -> 91.9 us
    all_gather x2 -> x0, blocking collectives: 36.5 us -> none  [apply_blocks(): lax.all_gather(panel, 'col', axis=0, tiled=True)]
    ppermute x0 -> x6, waiting for transfers between devices: none -> 13.9 us  [the longest x4 13.3 us: collect(): from_left = lax.ppermute(from_left, axis, right)]
    ppermute x0 -> x6, starting transfers between devices: none -> 8.37 us  [the longest x2 5.25 us: collect(): from_right = lax.ppermute(from_right, axis, left)]
    dynamic_update_slice x0 -> x7, local copies, waits for them, and re-layouts: none -> 5.56 us  [the longest x4 2.67 us: collect(): lax.dynamic_update_slice_in_dim(out, from_left, (index - step) % size * r...]
  transfers between devices with their start and end apart: 6 -> 12, of which waited for: 2 -> 6; matrix products, arithmetic and copies ran while one was open for 60% -> 65% of each run, Pallas kernels for 0% -> 0%
where the time goes in v1:
time: 243 us; the launch traced here: 242 us
  local copies, waits for them, and re-layouts  91.9 us (38%)
  matrix products  65.8 us (27%)
  waiting for transfers between devices  56.1 us (23%)
  between operations  14.3 us (6%)
  starting transfers between devices  9.02 us (4%)
  other arithmetic  4.77 us (2%)
    reduce_scatter x2, waiting for transfers between devices, apply_blocks(): lax.psum_scatter(upper_sum.reshape(range_blocks * BS, width), 'col', scat...  42.1 us
    dot_general x2, local copies, waits for them, and re-layouts, apply_blocks(): jnp.einsum('sij,sjw->siw', block_tiles, picked_set, preferred_element_typ...  25.6 us
    dot_general x2, local copies, waits for them, and re-layouts, apply_blocks(): jnp.einsum('sji,sjw->siw', block_tiles, picked_range, preferred_element_t...  25.5 us
    dot_general x2, matrix products, apply_blocks(): jnp.einsum('sij,sjw->siw', block_tiles, picked_set, preferred_element_typ...  18.9 us
    dot_general x2, matrix products, apply_blocks(): jnp.einsum('sji,sjw->siw', block_tiles, picked_range, preferred_element_t...  18.6 us
    gather x2, local copies, waits for them, and re-layouts, apply_blocks(): picked_set = jnp.take(gathered_set, set_slot, axis=0)  14.5 us
    dot_general x2, matrix products, apply_blocks(): jnp.einsum('as,siw->aiw', row_select, upper, precision=lax.Precision.HIGH...  14.2 us
    dot_general x2, matrix products, apply_blocks(): jnp.einsum('bs,siw->biw', set_select, lower, precision=lax.Precision.HIGH...  14.2 us
  transfers between devices with their start and end apart: 12, of which 6 were waited for; matrix products, arithmetic and copies ran while one was open for 65% of the time, Pallas kernels for 0%

profile of v1, /device:TPU:0, one launch (start us, length us, event | category | flops | bytes accessed | tf_op | source)
XLA Modules:
  0.0 241.9 jit_solution(5096583621111312540)
XLA Ops:
  6.5 3.1 %collective-permute-start = (bf16[256,256]{1,0:T(8,128)(2,1)}, bf16[256,256]{1,0:T(8,128)(2,1)S(1)}, u32[]{:S(2)}, u32[]{:S(2)}) collective-permute-start(bf16[256,256]{1,0:T(8,128)(2,1)} %param.9), channel_id=1, source_target_pairs={{0,1},{1,2},{2,3},{3,0},{4,5},{5,6},{6,7},{7,4},{8,9},{9,10},{10,1... | collective-permute-start | bytes 393224 | tf_op jit(solution)/shard_map/ppermute | solution.py:20
  9.6 2.0 collective-permute-start.1
  18.2 4.8 %collective-permute-done.2 = bf16[256,256]{1,0:T(8,128)(2,1)S(1)} collective-permute-done((bf16[256,256]{1,0:T(8,128)(2,1)S(1)}, bf16[256,256]{1,0:T(8,128)(2,1)S(1)}, u32[]{:S(2)}, u32[]{:S(2)}) %collective-permute-start.2) | collective-permute-done | bytes 131104 | tf_op jit(solution)/shard_map/ppermute | solution.py:20
  23.7 7.0 %gather_fusion.1 = bf16[96,128,256]{2,1,0:T(8,128)(2,1)} fusion(bf16[8,128,256]{2,1,0:T(8,128)(2,1)} %bitcast.6, s32[1024]{0:T(1024)S(1)} %pad_clamp_fusion), kind=kCustom, calls=%fused_computation.1.clone | custom fusion | bytes 12583296 | tf_op jit(solution)/shard_map/jit(_take)/gather | solution.py:46
  30.7 9.3 %fusion.12 = f32[96,256,128]{2,1,0:T(8,128)} fusion(bf16[96,128,128]{2,1,0:T(8,128)(2,1)S(1)} %copy-done, bf16[96,128,256]{2,1,0:T(8,128)(2,1)} %gather_fusion.1, pred[96]{0:T(512)(128)(4,1)S(1)} %get-tuple-element.11), kind=kOutput, calls=%fused_computation.16 | convolution fusion | flops 808452096 | bytes 22020192 | tf_op jit(solution)/shard_map/sji,sjw->siw/dot_general | solution.py:47
  40.0 12.7 %copy.11 = f32[96,256,128]{1,0,2:T(8,128)} copy(f32[96,256,128]{2,1,0:T(8,128)} %fusion.12) | data formatting | bytes 25165824 | tf_op jit(solution)/shard_map/sji,sjw->siw/dot_general | solution.py:47
  52.7 7.1 %fusion.24 = bf16[16,128,256]{2,0,1:T(8,128)(2,1)S(1)} fusion(f32[96,256,128]{1,0,2:T(8,128)} %copy.11, s32[96]{0:T(128)S(1)} %get-tuple-element.10, pred[96]{0:T(512)(128)(4,1)S(1)} %iota_compare_fusion.2), kind=kOutput, calls=%fused_computation.28 | convolution fusion | flops 604507136 | bytes 13631968 | tf_op jit(solution)/shard_map/bs,siw->biw/dot_general | solution.py:50
  61.4 7.3 %gather_fusion = bf16[96,128,256]{2,1,0:T(8,128)(2,1)} fusion(bf16[16,128,256]{2,1,0:T(8,128)(2,1)} %bitcast.42, s32[1024]{0:T(1024)S(1)} %pad_clamp_fusion.1), kind=kCustom, calls=%fused_computation.clone | custom fusion | bytes 12583296 | tf_op jit(solution)/shard_map/jit(_take)/gather | solution.py:37
  68.7 9.4 %fusion.14 = f32[96,256,128]{2,1,0:T(8,128)} fusion(bf16[96,128,128]{2,1,0:T(8,128)(2,1)S(1)} %copy-done, bf16[96,128,256]{2,1,0:T(8,128)(2,1)} %gather_fusion, pred[96]{0:T(512)(128)(4,1)S(1)} %get-tuple-element.9), kind=kOutput, calls=%fused_computation.18 | convolution fusion | flops 808452096 | bytes 22020192 | tf_op jit(solution)/shard_map/sij,sjw->siw/dot_general | solution.py:38
  78.2 12.8 %copy.10 = f32[96,256,128]{1,0,2:T(8,128)} copy(f32[96,256,128]{2,1,0:T(8,128)} %fusion.14) | data formatting | bytes 25165824 | tf_op jit(solution)/shard_map/sij,sjw->siw/dot_general | solution.py:38
  90.9 7.1 %fusion.30 = bf16[8,128,256]{2,0,1:T(8,128)(2,1)S(1)} fusion(f32[96,256,128]{1,0,2:T(8,128)} %copy.10, s32[96]{0:T(128)S(1)} %get-tuple-element.12, pred[96]{0:T(512)(128)(4,1)S(1)} %iota_compare_fusion.2), kind=kOutput, calls=%fused_computation.30 | convolution fusion | flops 302253568 | bytes 13107680 | tf_op jit(solution)/shard_map/as,siw->aiw/dot_general | solution.py:39
  99.1 21.7 %reduce-scatter.5.cloned.1.call-done = bf16[256,256]{1,0:T(8,128)(2,1)} async-done(((bf16[1024,256]{1,0:T(8,128)(2,1)}), bf16[256,256]{1,0:T(8,128)(2,1)}) %reduce-scatter.5.cloned.1.call-update) | async-done | bytes 131088 | tf_op jit(solution)/shard_map/reduce_scatter | solution.py:42
  124.1 3.2 %collective-permute-start.4 = (bf16[256,256]{1,0:T(8,128)(2,1)}, bf16[256,256]{1,0:T(8,128)(2,1)S(1)}, u32[]{:S(2)}, u32[]{:S(2)}) collective-permute-start(bf16[256,256]{1,0:T(8,128)(2,1)} %copy-done.2), channel_id=1, source_target_pairs={{0,3},{1,0},{2,1},{3,2},{4,7},{5,4},{6,5},{7,6},{8,11},{9,8},{10,9... | collective-permute-start | bytes 393224 | tf_op jit(solution)/shard_map/ppermute | solution.py:25
  127.3 3.0 %collective-permute-done.3 = bf16[256,256]{1,0:T(8,128)(2,1)S(1)} collective-permute-done((bf16[256,256]{1,0:T(8,128)(2,1)S(1)}, bf16[256,256]{1,0:T(8,128)(2,1)S(1)}, u32[]{:S(2)}, u32[]{:S(2)}) %collective-permute-start.3) | collective-permute-done | bytes 131104 | tf_op jit(solution)/shard_map/ppermute | solution.py:20
  131.6 5.4 %collective-permute-done.5 = bf16[256,256]{1,0:T(8,128)(2,1)S(1)} collective-permute-done((bf16[256,256]{1,0:T(8,128)(2,1)S(1)}, bf16[256,256]{1,0:T(8,128)(2,1)S(1)}, u32[]{:S(2)}, u32[]{:S(2)}) %collective-permute-start.5) | collective-permute-done | bytes 131104 | tf_op jit(solution)/shard_map/ppermute | solution.py:20
  137.7 7.0 %gather_fusion.3 = bf16[96,128,256]{2,1,0:T(8,128)(2,1)} fusion(bf16[8,128,256]{2,1,0:T(8,128)(2,1)} %bitcast.12, s32[1024]{0:T(1024)S(1)} %pad_clamp_fusion), kind=kCustom, calls=%fused_computation.3.clone | custom fusion | bytes 12583296 | tf_op jit(solution)/shard_map/jit(_take)/gather | solution.py:46
  144.7 9.3 %fusion.8 = f32[96,256,128]{2,1,0:T(8,128)} fusion(bf16[96,128,128]{2,1,0:T(8,128)(2,1)S(1)} %copy-done, bf16[96,128,256]{2,1,0:T(8,128)(2,1)} %gather_fusion.3, pred[96]{0:T(512)(128)(4,1)S(1)} %get-tuple-element.11), kind=kOutput, calls=%fused_computation.12 | convolution fusion | flops 808452096 | bytes 22020192 | tf_op jit(solution)/shard_map/sji,sjw->siw/dot_general | solution.py:47
  154.0 12.7 %copy.13 = f32[96,256,128]{1,0,2:T(8,128)} copy(f32[96,256,128]{2,1,0:T(8,128)} %fusion.8) | data formatting | bytes 25165824 | tf_op jit(solution)/shard_map/sji,sjw->siw/dot_general | solution.py:47
  166.7 7.1 %fusion.27 = bf16[16,128,256]{2,0,1:T(8,128)(2,1)S(1)} fusion(f32[96,256,128]{1,0,2:T(8,128)} %copy.13, s32[96]{0:T(128)S(1)} %copy-done.9, pred[96]{0:T(512)(128)(4,1)S(1)} %iota_compare_fusion.2), kind=kOutput, calls=%fused_computation.29 | convolution fusion | flops 604507136 | bytes 13631968 | tf_op jit(solution)/shard_map/bs,siw->biw/dot_general | solution.py:50
  175.6 7.3 %gather_fusion.2 = bf16[96,128,256]{2,1,0:T(8,128)(2,1)} fusion(bf16[16,128,256]{2,1,0:T(8,128)(2,1)} %bitcast.43, s32[1024]{0:T(1024)S(1)} %pad_clamp_fusion.1), kind=kCustom, calls=%fused_computation.2.clone | custom fusion | bytes 12583296 | tf_op jit(solution)/shard_map/jit(_take)/gather | solution.py:37
  182.8 9.4 %fusion.10 = f32[96,256,128]{2,1,0:T(8,128)} fusion(bf16[96,128,128]{2,1,0:T(8,128)(2,1)S(1)} %copy-done, bf16[96,128,256]{2,1,0:T(8,128)(2,1)} %gather_fusion.2, pred[96]{0:T(512)(128)(4,1)S(1)} %copy-done.7), kind=kOutput, calls=%fused_computation.14 | convolution fusion | flops 808452096 | bytes 22020192 | tf_op jit(solution)/shard_map/sij,sjw->siw/dot_general | solution.py:38
  192.2 12.8 %copy.12 = f32[96,256,128]{1,0,2:T(8,128)} copy(f32[96,256,128]{2,1,0:T(8,128)} %fusion.10) | data formatting | bytes 25165824 | tf_op jit(solution)/shard_map/sij,sjw->siw/dot_general | solution.py:38
  205.1 7.0 %fusion.33 = bf16[8,128,256]{2,0,1:T(8,128)(2,1)S(1)} fusion(f32[96,256,128]{1,0,2:T(8,128)} %copy.12, s32[96]{0:T(128)S(1)} %copy-done.5, pred[96]{0:T(512)(128)(4,1)S(1)} %iota_compare_fusion.2), kind=kOutput, calls=%fused_computation.31 | convolution fusion | flops 302253568 | bytes 13107680 | tf_op jit(solution)/shard_map/as,siw->aiw/dot_general | solution.py:39
  213.1 20.3 %reduce-scatter.9.cloned.1.call-done = bf16[256,256]{1,0:T(8,128)(2,1)} async-done(((bf16[1024,256]{1,0:T(8,128)(2,1)}), bf16[256,256]{1,0:T(8,128)(2,1)}) %reduce-scatter.9.cloned.1.call-update) | async-done | bytes 131088 | tf_op jit(solution)/shard_map/reduce_scatter | solution.py:42
  (64 shorter events, 18.7 us)
Async XLA Ops:
  6.5 24.1 %copy-start = (bf16[96,128,128]{2,1,0:T(8,128)(2,1)S(1)}, bf16[96,128,128]{2,1,0:T(8,128)(2,1)}, u32[]{:S(2)}) copy-start(bf16[96,128,128]{2,1,0:T(8,128)(2,1)} %param.10) | copy-start | bytes 9437188
  6.5 54.9 %all-gather.3.cloned.1.call-start = ((), (), s32[]{:S(2)}) async-start(), calls=%async_computation.4 | async-start | bytes 1179648 | tf_op jit(solution)/shard_map/all_gather | solution.py:36
  6.5 9.7 %collective-permute-start = (bf16[256,256]{1,0:T(8,128)(2,1)}, bf16[256,256]{1,0:T(8,128)(2,1)S(1)}, u32[]{:S(2)}, u32[]{:S(2)}) collective-permute-start(bf16[256,256]{1,0:T(8,128)(2,1)} %param.9), channel_id=1, source_target_pairs={{0,1},{1,2},{2,3},{3,0},{4,5},{5,6},{6,7},{7,4},{8,9},{9,10},{10,1... | collective-permute-start | bytes 393224 | tf_op jit(solution)/shard_map/ppermute | solution.py:20
  9.6 8.0 %collective-permute-start.1 = (bf16[256,256]{1,0:T(8,128)(2,1)}, bf16[256,256]{1,0:T(8,128)(2,1)S(1)}, u32[]{:S(2)}, u32[]{:S(2)}) collective-permute-start(bf16[256,256]{1,0:T(8,128)(2,1)} %param.9), channel_id=1, source_target_pairs={{0,3},{1,0},{2,1},{3,2},{4,7},{5,4},{6,5},{7,6},{8,11},{9,8},{10,9... | collective-permute-start | bytes 393224 | tf_op jit(solution)/shard_map/ppermute | solution.py:25
  11.6 87.4 %reduce-scatter.7.cloned.1.call-start = ((), (), s32[]{:S(2)}) async-start(), calls=%async_computation.6 | async-start | bytes 1179648 | tf_op jit(solution)/shard_map/reduce_scatter | solution.py:53
  12.4 78.6 %copy-start.4 = (s32[96]{0:T(128)}, s32[96]{0:T(128)S(1)}, u32[]{:S(2)}) copy-start(s32[96]{0:T(128)S(1)} %get-tuple-element.12) | copy-start | bytes 1156
  13.1 48.3 %copy-start.8 = (s32[96]{0:T(128)}, s32[96]{0:T(128)S(1)}, u32[]{:S(2)}) copy-start(s32[96]{0:T(128)S(1)} %get-tuple-element.10) | copy-start | bytes 1156
  13.1 55.7 %copy-start.6 = (pred[96]{0:T(512)(128)(4,1)}, pred[96]{0:T(512)(128)(4,1)S(1)}, u32[]{:S(2)}) copy-start(pred[96]{0:T(512)(128)(4,1)S(1)} %get-tuple-element.9) | copy-start | bytes 292
  16.2 6.8 %collective-permute-start.2 = (bf16[256,256]{1,0:T(8,128)(2,1)S(1)}, bf16[256,256]{1,0:T(8,128)(2,1)S(1)}, u32[]{:S(2)}, u32[]{:S(2)}) collective-permute-start(bf16[256,256]{1,0:T(8,128)(2,1)S(1)} %collective-permute-done), channel_id=1, source_target_pairs={{0,1},{1,2},{2,3},{3,0},{4,5},{5,6},{6,7},{7,4},{8,9},{9,10},{10,1... | collective-permute-start | bytes 393224 | tf_op jit(solution)/shard_map/ppermute | solution.py:20
  61.1 59.7 %reduce-scatter.5.cloned.1.call-start = ((), (), s32[]{:S(2)}) async-start(), calls=%async_computation.5 | async-start | bytes 655360 | tf_op jit(solution)/shard_map/reduce_scatter | solution.py:42
  90.9 30.7 %copy-start.1 = (bf16[256,256]{1,0:T(8,128)(2,1)S(1)}, bf16[256,256]{1,0:T(8,128)(2,1)}, u32[]{:S(2)}) copy-start(bf16[256,256]{1,0:T(8,128)(2,1)} %param.9) | copy-start | bytes 393220
  99.0 76.5 %all-gather.5.cloned.1.call-start = ((), (), s32[]{:S(2)}) async-start(), calls=%async_computation.7 | async-start | bytes 1179648 | tf_op jit(solution)/shard_map/all_gather | solution.py:36
  123.3 0.7 copy-start.2
  123.3 7.0 %collective-permute-start.3 = (bf16[256,256]{1,0:T(8,128)(2,1)S(1)}, bf16[256,256]{1,0:T(8,128)(2,1)S(1)}, u32[]{:S(2)}, u32[]{:S(2)}) collective-permute-start(bf16[256,256]{1,0:T(8,128)(2,1)S(1)} %get-tuple-element.8), channel_id=1, source_target_pairs={{0,1},{1,2},{2,3},{3,0},{4,5},{5,6},{6,7},{7,4},{8,9},{9,10},{10,1... | collective-permute-start | bytes 393224 | tf_op jit(solution)/shard_map/ppermute | solution.py:20
  124.0 89.0 %reduce-scatter.11.cloned.1.call-start = ((), (), s32[]{:S(2)}) async-start(), calls=%async_computation.9 | async-start | bytes 1179648 | tf_op jit(solution)/shard_map/reduce_scatter | solution.py:53
  124.1 6.9 %collective-permute-start.4 = (bf16[256,256]{1,0:T(8,128)(2,1)}, bf16[256,256]{1,0:T(8,128)(2,1)S(1)}, u32[]{:S(2)}, u32[]{:S(2)}) collective-permute-start(bf16[256,256]{1,0:T(8,128)(2,1)} %copy-done.2), channel_id=1, source_target_pairs={{0,3},{1,0},{2,1},{3,2},{4,7},{5,4},{6,5},{7,6},{8,11},{9,8},{10,9... | collective-permute-start | bytes 393224 | tf_op jit(solution)/shard_map/ppermute | solution.py:25
  130.3 6.8 %collective-permute-start.5 = (bf16[256,256]{1,0:T(8,128)(2,1)S(1)}, bf16[256,256]{1,0:T(8,128)(2,1)S(1)}, u32[]{:S(2)}, u32[]{:S(2)}) collective-permute-start(bf16[256,256]{1,0:T(8,128)(2,1)S(1)} %collective-permute-done.3), channel_id=1, source_target_pairs={{0,1},{1,2},{2,3},{3,0},{4,5},{5,6},{6,7},{7,4},{8,9},{9,10},{10,1... | collective-permute-start | bytes 393224 | tf_op jit(solution)/shard_map/ppermute | solution.py:20
  154.0 12.7 %copy-start.9 = (s32[96]{0:T(128)S(1)}, s32[96]{0:T(128)}, u32[]{:S(2)}) copy-start(s32[96]{0:T(128)} %copy-done.8) | copy-start | bytes 1156
  175.2 58.2 %reduce-scatter.9.cloned.1.call-start = ((), (), s32[]{:S(2)}) async-start(), calls=%async_computation.8 | async-start | bytes 655360 | tf_op jit(solution)/shard_map/reduce_scatter | solution.py:42
  175.5 7.3 %copy-start.7 = (pred[96]{0:T(512)(128)(4,1)S(1)}, pred[96]{0:T(512)(128)(4,1)}, u32[]{:S(2)}) copy-start(pred[96]{0:T(512)(128)(4,1)} %copy-done.6) | copy-start | bytes 292
  192.2 12.8 %copy-start.5 = (s32[96]{0:T(128)S(1)}, s32[96]{0:T(128)}, u32[]{:S(2)}) copy-start(s32[96]{0:T(128)} %copy-done.4) | copy-start | bytes 1156
  205.1 28.3 %copy-start.3 = (bf16[256,256]{1,0:T(8,128)(2,1)S(1)}, bf16[256,256]{1,0:T(8,128)(2,1)}, u32[]{:S(2)}) copy-start(bf16[256,256]{1,0:T(8,128)(2,1)} %copy-done.2) | copy-start | bytes 393220
Sparse Core Ops, SparseCore 0:
  11.8 23.5 all-gather.2
  61.3 35.3 reduce-scatter.6
  99.1 21.6 reduce-scatter.4
  124.1 23.9 all-gather.4
  175.3 34.0 reduce-scatter.10
  213.2 20.1 reduce-scatter.8
